TPU v7x, 32 devices: a whole 2x2x4 slice. The times are simulated.
32 devices in a mesh: shard: 4 (over z), ctx: 2 (over y), tp: 4 (over x, core).
Axes of the slice: x: 2, y: 2, z: 4, core: 2. Of those that a mesh axis runs over, the one named last changes fastest.
Arguments:
- inputs: bfloat16 [16, 1024, 512], P('shard', 'ctx'), may hold values from -6 to 6
- first_memory: float32 [16, 64, 512], P('shard'), may hold values from -6 to 6
- piece_start: int32 [16, 2], P('shard', 'ctx'), may hold values from 0 to 448, as said below
- piece_len: int32 [16, 2], P('shard', 'ctx'), may hold values from 64 to 256, as said below
- w_query: bfloat16 [512, 512], P(('shard', 'tp')), may hold values from -0.25 to 0.25
- w_key: bfloat16 [512, 512], P(('shard', 'tp')), may hold values from -0.25 to 0.25
- w_value: bfloat16 [512, 512], P(('shard', 'tp')), may hold values from -0.25 to 0.25
- w_out: bfloat16 [512, 512], P(('shard', 'tp')), may hold values from -1 to 1
- w_up: bfloat16 [512, 2048], P(('shard', 'tp')), may hold values from -0.25 to 0.25
- w_down: bfloat16 [2048, 512], P(('shard', 'tp')), may hold values from -0.125 to 0.125
- u_query: bfloat16 [512, 512], P(('shard', 'tp')), may hold values from -0.25 to 0.25
- u_key: bfloat16 [512, 512], P(('shard', 'tp')), may hold values from -0.25 to 0.25
- u_value: bfloat16 [512, 512], P(('shard', 'tp')), may hold values from -0.25 to 0.25
- u_out: bfloat16 [512, 512], P(('shard', 'tp')), may hold values from -1 to 1
- u_gate: bfloat16 [512, 512], P(('shard', 'tp')), may hold values from -0.25 to 0.25
- gain_attn: float32 [512], replicated, may hold values from 0.5 to 1.5
- gain_ffn: float32 [512], replicated, may hold values from 0.5 to 1.5
- gain_write: float32 [512], replicated, may hold values from 0.5 to 1.5
- gate_bias: float32 [512], replicated, may hold values from 1 to 3
- out_grad: bfloat16 [16, 1024, 512], P('shard', ('ctx', 'tp')), may hold values from -6 to 6
- memory_grad: float32 [16, 128, 512], P('shard', 'ctx'), may hold values from -6 to 6
Outputs:
- outputs: bfloat16 [16, 1024, 512], P('shard', ('ctx', 'tp'))
- memories_after: float32 [16, 128, 512], P('shard', 'ctx')
- input_grad: bfloat16 [16, 1024, 512], P('shard', ('ctx', 'tp'))
- memory_in_grad: float32 [16, 128, 512], P('shard', 'ctx')
- grad_w_query: float32 [512, 512], P(('shard', 'ctx'), 'tp')
- grad_w_key: float32 [512, 512], P(('shard', 'ctx'), 'tp')
- grad_w_value: float32 [512, 512], P(('shard', 'ctx'), 'tp')
- grad_w_out: float32 [512, 512], P(('shard', 'ctx', 'tp'))
- grad_w_up: float32 [512, 2048], P(('shard', 'ctx', 'tp'))
- grad_w_down: float32 [2048, 512], P(('shard', 'ctx', 'tp'))
- grad_u_query: float32 [512, 512], P(('shard', 'ctx'), 'tp')
- grad_u_key: float32 [512, 512], P(('shard', 'ctx'), 'tp')
- grad_u_value: float32 [512, 512], P(('shard', 'ctx'), 'tp')
- grad_u_out: float32 [512, 512], P('tp', ('shard', 'ctx'))
- grad_u_gate: float32 [512, 512], P('tp', ('shard', 'ctx'))
- grad_gain_attn: float32 [512], P(('shard', 'ctx', 'tp'))
- grad_gain_ffn: float32 [512], P(('shard', 'ctx', 'tp'))
- grad_gain_write: float32 [512], P(('shard', 'ctx', 'tp'))
- grad_gate_bias: float32 [512], P(('shard', 'ctx', 'tp'))
Inputs may be any that keep to these rules, and one draw needn't show every extreme that they name: `piece_len`: each segment has one picture piece of 64 to 256 tokens; some piece has exactly 256. A piece lies inside its segment: piece_start + piece_len <= 512.
All inputs are finite; a program needn't handle non-finite values.
Results may differ from a plain program's by a relative error of at most 0.03.
Values may be sent and summed in bfloat16 or wider, within the bound.
A program may use at most 128 MiB of HBM per device.

v0:
```python
from functools import partial

import jax
import jax.numpy as jnp
from jax import lax
from jax.experimental import pallas as pl
from jax.experimental.pallas import tpu as pltpu
from jax.sharding import PartitionSpec as P

F32 = jnp.float32
BF = jnp.bfloat16
MESH = pl.DeviceIdType.MESH
HEAD = 64
EPS = 1e-05
NEG = -1e30
VMEM_LIMIT = 67000000

WQ, WK, WV, WO, WUP, WDOWN, UQ, UK, UV, UO, UGATE = 0, 1, 2, 3, 4, 8, 12, 13, 14, 15, 16
TILES = 17


def dot(a, b):
    return lax.dot_general(a, b, (((1,), (0,)), ((), ())), preferred_element_type=F32)


def dot_nt(a, b):
    return lax.dot_general(a, b, (((1,), (1,)), ((), ())), preferred_element_type=F32)


def dot_tn(a, b):
    return lax.dot_general(a, b, (((0,), (0,)), ((), ())), preferred_element_type=F32)


def rows_at(i, size):
    return pl.ds(pl.multiple_of(i * size, size), size)


def loop(count, unroll=1):
    def run(body):
        def step(i, carry):
            body(i)
            return carry

        lax.fori_loop(0, count, step, 0, unroll=unroll)

    return run


BLOCK = 64
UNROLL = 4


def blocks(total, body, carry=None):
    def step(n, carry):
        for k in range(UNROLL):
            i = n * UNROLL + k
            carry = body(rows_at(i, BLOCK), i, carry)
        return carry

    return lax.fori_loop(0, total // (BLOCK * UNROLL), step, carry)


def fold(values):
    return jnp.sum(values.reshape(values.shape[0] // 8, 8, values.shape[1]), axis=0)


def normed(v):
    mean = jnp.mean(v, axis=-1, keepdims=True)
    centered = v - mean
    inv = lax.rsqrt(jnp.mean(centered * centered, axis=-1, keepdims=True) + EPS)
    return centered * inv, inv


def norm_pull(e, gain, hat, inv):
    h = e * gain
    m0 = jnp.mean(h, axis=-1, keepdims=True)
    m1 = jnp.mean(h * hat, axis=-1, keepdims=True)
    return inv * (h - m0 - hat * m1)


def lane_block(width, block):
    return lax.broadcasted_iota(jnp.int32, (1, width), 1) // block


class Weights:
    def __init__(self, ref):
        self.ref = ref
        self.blocks, _, self.rows, self.width = ref.shape

    def cols(self, tile, start, size):
        got = self.ref[:, tile, :, pl.ds(start, size)]
        return got.reshape(self.blocks * self.rows, size)

    def row_part(self, tile, part, parts):
        count = self.blocks // parts
        got = self.ref[pl.ds(part * count, count), tile]
        return got.reshape(count * self.rows, self.width)

    def down_cols(self, chunk, chunks, start, size):
        count = self.blocks // chunks
        got = self.ref[pl.ds(chunk * count, count), WDOWN : WDOWN + 4, :, pl.ds(start, size)]
        return got.reshape(count * 4 * self.rows, size)

    def down_rows(self, part, parts):
        count = self.blocks // parts
        got = self.ref[pl.ds(part * count, count), WDOWN : WDOWN + 4]
        return got.reshape(count * 4 * self.rows, self.width)


def unit_scratch(tokens, slots, width, ff):
    r = tokens + slots
    heads = width // HEAD
    quads = width // 256
    v = pltpu.VMEM
    return dict(
        mem=v((slots, width), F32),
        xh=v((r, width), F32),
        xr=v((r, 1), F32),
        enc=v((r, width), BF),
        q=v((tokens, width), BF),
        k=v((r, width), BF),
        v=v((r, width), BF),
        kt=v((width, r), BF),
        vt=v((width, r), BF),
        pt=v((heads, r, tokens), BF),
        ptop=v((heads, 1, tokens), F32),
        psum=v((heads, 1, tokens), F32),
        pinv=v((heads, 1, tokens), F32),
        top=v((2, 1, 256), F32),
        mixt=v((width, tokens), BF),
        af=v((r, width), F32),
        ah=v((tokens, width), F32),
        ar=v((tokens, 1), F32),
        fin=v((tokens, width), BF),
        act=v((ff // 512, tokens, 512), BF),
        dg=v((ff // 512, tokens, 512), BF),
        yh=v((tokens, width), F32),
        yr=v((tokens, 1), F32),
        wri=v((r, width), BF),
        sq=v((slots, width), BF),
        sk=v((r, width), BF),
        sv=v((r, width), BF),
        spt=v((quads, r, 256), BF),
        wrt=v((slots, width), BF),
        gate=v((slots, width), F32),
        f1=v((slots, width), F32),
        f2=v((slots, width), F32),
        gm=v((slots, width), F32),
        gup=v((slots, width), BF),
        ggl=v((slots, width), BF),
        dsq=v((slots, width), BF),
        dsk=v((r, width), BF),
        dsv=v((r, width), BF),
        e=v((r, width), F32),
        gy=v((tokens, width), F32),
        gyb=v((tokens, width), BF),
        bwm=v((slots, width), F32),
        gpre=v((ff // 512, tokens, 512), BF),
        gab=v((tokens, width), BF),
        gmx=v((tokens, width), BF),
        dst=v((2, r, tokens), BF),
        dqt=v((width, tokens), BF),
        dq=v((tokens, width), BF),
        dk=v((r, width), BF),
        dv=v((r, width), BF),
    )


class Unit:
    def __init__(self, refs, w, x, gains, small):
        self.__dict__.update(refs)
        self.w = w
        self.x = x
        self.gains = gains
        self.small = small
        self.tokens, self.width = x.shape
        self.slots = self.mem.shape[0]
        self.r = self.tokens + self.slots
        self.ff = self.act.shape[0] * 512

    def gain(self, i):
        return self.gains[i][...]

    def make_bias(self, first, length):
        t = self.tokens

        @loop(t // 64)
        def _(i):
            key = lax.broadcasted_iota(jnp.int32, (64, t), 0) + i * 64
            query = lax.broadcasted_iota(jnp.int32, (64, t), 1)
            last = first + length
            inside = (key >= first) & (key < last) & (query >= first) & (query < last)
            seen = (key <= query) | inside
            self.e[rows_at(i, 64), :] = jnp.where(seen, 0.0, NEG).astype(F32)

    def norm_in(self, rows, values):
        hat, inv = normed(values)
        self.xh[rows, :] = hat
        self.xr[rows, :] = inv
        self.enc[rows, :] = (hat * self.gain(0)).astype(BF)

    def tokens_in(self):
        def body(rows, i, carry):
            self.norm_in(rows, self.x[rows, :].astype(F32))

        blocks(self.tokens, body)

    def project_tokens(self):
        t = self.tokens

        @loop(self.width // 256)
        def _(n):
            cols = rows_at(n, 256)
            enc = self.enc[0:t, :]
            got = dot(enc, self.w.cols(WQ, n * 256, 256)).astype(BF)
            self.q[:, cols] = got * BF(HEAD**-0.5)
            self.k[0:t, cols] = dot(enc, self.w.cols(WK, n * 256, 256)).astype(BF)
            self.v[0:t, cols] = dot(enc, self.w.cols(WV, n * 256, 256)).astype(BF)

        self.vt[:, 0:t] = self.v[0:t, :].T

    def memory_in(self):
        t, r = self.tokens, self.r
        self.norm_in(slice(t, r), self.mem[...])
        enc = self.enc[t:r, :]
        self.k[t:r, :] = dot(enc, self.w.cols(WK, 0, self.width)).astype(BF)
        self.v[t:r, :] = dot(enc, self.w.cols(WV, 0, self.width)).astype(BF)
        self.vt[:, t:r] = self.v[t:r, :].T

    def held(self, j):
        return self.af.at[:, j % 2 * 256 : j % 2 * 256 + 256]

    def attend(self, first, count):
        t = self.tokens
        span = 256

        @loop(count)
        def _(i):
            p = i + first
            cols = rows_at(p, 128)
            half = lane_block(128, HEAD)
            steps = [(hh, n) for hh in range(2) for n in range(t // span)]

            def score(j):
                hh, n = steps[j]
                qc = slice(n * span, n * span + span)
                q = self.q[qc, cols]
                s = dot_nt(self.k[0:t, cols], jnp.where(half == hh, q, jnp.zeros_like(q)))
                part = s[n * span : t] + self.e[n * span : t, qc]
                top = jnp.max(part, axis=0, keepdims=True)
                self.held(j)[n * span : t, :] = part
                if n > 0:
                    self.held(j)[0 : n * span, :] = s[0 : n * span]
                    top = jnp.maximum(top, jnp.max(s[0 : n * span], axis=0, keepdims=True))
                self.ptop[2 * p + hh, :, qc] = top

            def soften(j):
                hh, n = steps[j]
                qc = slice(n * span, n * span + span)
                e = jnp.exp(self.held(j)[0:t, :] - self.ptop[2 * p + hh, :, qc])
                self.psum[2 * p + hh, :, qc] = jnp.sum(e, axis=0, keepdims=True)
                self.pt[2 * p + hh, 0:t, qc] = e.astype(BF)

            def mix(j):
                hh, n = steps[j]
                qc = slice(n * span, n * span + span)
                feats = pl.ds(pl.multiple_of(p * 128 + hh * HEAD, HEAD), HEAD)
                self.yh[feats, qc] = dot(self.vt[feats, 0:t], self.pt[2 * p + hh, 0:t, qc])

            score(0)
            for j in range(len(steps)):
                if j + 1 < len(steps):
                    score(j + 1)
                soften(j)
                mix(j)

    def attend_memory(self):
        t, r = self.tokens, self.r

        @loop(self.width // 128)
        def _(p):
            cols = rows_at(p, 128)
            half = lane_block(128, HEAD)
            for hh in range(2):
                h = 2 * p + hh
                feats = pl.ds(pl.multiple_of(p * 128 + hh * HEAD, HEAD), HEAD)
                q = self.q[:, cols]
                s = dot_nt(self.k[t:r, cols], jnp.where(half == hh, q, jnp.zeros_like(q)))
                top = jnp.maximum(self.ptop[h], jnp.max(s, axis=0, keepdims=True))
                fade = jnp.exp(self.ptop[h] - top)
                e = jnp.exp(s - top)
                inv = 1.0 / (fade * self.psum[h] + jnp.sum(e, axis=0, keepdims=True))
                self.pinv[h] = inv
                low = e.astype(BF)
                self.pt[h, t:r, :] = low
                got = self.yh[feats, :] * fade + dot(self.vt[feats, t:r], low)
                self.mixt[feats, :] = (got * inv).astype(BF)
                for m in range(t // 64):
                    rows = slice(m * 64, m * 64 + 64)
                    self.pt[h, rows, :] = (self.pt[h, rows, :].astype(F32) * fade).astype(BF)

    def after_attention(self):
        t = self.tokens
        self.gmx[...] = self.mixt[...].T

        @loop(self.width // 256)
        def _(n):
            cols = rows_at(n, 256)
            got = dot(self.gmx[...], self.w.cols(WO, n * 256, 256))
            self.af[0:t, cols] = self.x[:, cols].astype(F32) + got

        def body(rows, i, carry):
            hat, inv = normed(self.af[rows, :])
            self.ah[rows, :] = hat
            self.ar[rows, :] = inv
            self.fin[rows, :] = (hat * self.gain(1)).astype(BF)

        blocks(t, body)

    def feed_forward_up(self, first, count):
        t = self.tokens
        c = 0.7978845608028654

        @loop(count)
        def _(i):
            j = i + first

            def project(n):
                part = slice(n * 256, n * 256 + 256)
                self.gy[:, part] = dot(self.fin[...], self.w.cols(WUP + j, n * 256, 256))

            def activate(n):
                part = slice(n * 256, n * 256 + 256)
                for m in range(t // 64):
                    rows = slice(m * 64, m * 64 + 64)
                    pre = self.gy[rows, part]
                    sq = pre * pre
                    th = jnp.tanh(pre * (c + (c * 0.044715) * sq))
                    half = 0.5 + 0.5 * th
                    self.act[j, rows, part] = (pre * half).astype(BF)
                    slope = half + (0.5 * pre) * (1.0 - th * th) * (c + (3 * c * 0.044715) * sq)
                    self.dg[j, rows, part] = slope.astype(BF)

            project(0)
            project(1)
            activate(0)
            activate(1)

    def feed_forward_down(self):
        t = self.tokens

        @loop(self.width // 256)
        def _(n):
            cols = rows_at(n, 256)
            total = self.af[0:t, cols]
            for j in range(self.ff // 512):
                total = total + dot(
                    self.act[j], self.w.down_cols(j, self.ff // 512, n * 256, 256)
                )
            self.af[0:t, cols] = total

        def body(rows, i, carry):
            hat, inv = normed(self.af[rows, :])
            self.yh[rows, :] = hat
            self.yr[rows, :] = inv
            self.wri[rows, :] = (hat * self.gain(2)).astype(BF)

        blocks(t, body)

        self.wri[t : self.r, :] = (self.xh[t : self.r, :] * self.gain(2)).astype(BF)

    def spread_heads(self, rows, g):
        part = rows[:, g * 256 : g * 256 + 256]
        block = lane_block(256, HEAD)
        return jnp.concatenate(
            [jnp.where(block == h, part, jnp.zeros_like(part)) for h in range(4)], axis=0
        )

    def gather_heads(self, stacked):
        block = lane_block(256, HEAD)
        s = self.slots
        total = jnp.where(block == 0, stacked[0:s], 0.0)
        for h in range(1, 4):
            total = total + jnp.where(block == h, stacked[h * s : h * s + s], 0.0)
        return total

    def write_memory(self):
        t, r = self.tokens, self.r

        @loop(self.width // 256)
        def _(n):
            cols = rows_at(n, 256)
            wri = self.wri[...]
            self.sk[:, cols] = dot(wri, self.w.cols(UK, n * 256, 256)).astype(BF)
            self.sv[:, cols] = dot(wri, self.w.cols(UV, n * 256, 256)).astype(BF)

        wm = self.wri[t:r, :]
        sq = dot(wm, self.w.cols(UQ, 0, self.width)).astype(BF)
        self.sq[...] = sq * BF(HEAD**-0.5)
        for g in range(self.width // 256):
            cols = slice(g * 256, g * 256 + 256)
            s = dot_nt(self.sk[:, cols], self.spread_heads(self.sq[...], g))
            e = jnp.exp(s - jnp.max(s, axis=0, keepdims=True))
            probs = (e * (1.0 / jnp.sum(e, axis=0, keepdims=True))).astype(BF)
            self.spt[g] = probs
            self.wrt[:, cols] = self.gather_heads(dot_tn(probs, self.sv[:, cols])).astype(BF)
        th = jnp.tanh(dot(self.wrt[...], self.w.cols(UO, 0, self.width)))
        pre = dot(wm, self.w.cols(UGATE, 0, self.width))
        gate = jax.nn.sigmoid(pre + self.gain(3))
        mem = self.mem[...]
        self.gate[...] = gate
        self.f1[...] = (mem - th) * gate * (1.0 - gate)
        self.f2[...] = (1.0 - gate) * (1.0 - th * th)
        return gate * mem + (1.0 - gate) * th

    def backward_early(self):
        self.kt[...] = self.k[...].T

    def write_back(self):
        gm = self.gm[...]
        ggp = gm * self.f1[...]
        gup = (gm * self.f2[...]).astype(BF)
        ggl = ggp.astype(BF)
        self.gup[...] = gup
        self.ggl[...] = ggl
        self.small[3:4, :] = jnp.sum(ggp, axis=0, keepdims=True)
        gwr = dot_nt(gup, self.w.row_part(UO, 0, 1)).astype(BF)
        quads = range(self.width // 256)
        cols = [slice(g * 256, g * 256 + 256) for g in quads]
        grads = [self.spread_heads(gwr, g) for g in quads]
        for g in quads:
            self.af[:, cols[g]] = dot_nt(self.sv[:, cols[g]], grads[g])
        for g in quads:
            self.dsv[:, cols[g]] = dot(self.spt[g], grads[g]).astype(BF)
        for g in quads:
            pf = self.spt[g].astype(F32)
            dp = self.af[:, cols[g]]
            self.dst[0, :, cols[g]] = (pf * (dp - jnp.sum(pf * dp, axis=0, keepdims=True))).astype(BF)
        for g in quads:
            dq = self.gather_heads(dot_tn(self.dst[0, :, cols[g]], self.sk[:, cols[g]])) * HEAD**-0.5
            self.dsq[:, cols[g]] = dq.astype(BF)
            self.dsk[:, cols[g]] = dot(self.dst[0, :, cols[g]], self.spread_heads(self.sq[...], g)).astype(BF)

    def write_enter(self, out_grad):
        t, r = self.tokens, self.r

        @loop(2)
        def _(n):
            cols = rows_at(n, self.width // 2)
            self.e[:, cols] = dot_nt(self.dsk[...], self.w.row_part(UK, n, 2)) + dot_nt(
                self.dsv[...], self.w.row_part(UV, n, 2)
            )

        em = self.e[t:r, :] + dot_nt(self.dsq[...], self.w.row_part(UQ, 0, 1))
        em = em + dot_nt(self.ggl[...], self.w.row_part(UGATE, 0, 1))
        hat = self.xh[t:r, :]
        self.bwm[...] = norm_pull(em, self.gain(2), hat, self.xr[t:r, :])

        def body(rows, i, carry):
            e = self.e[rows, :]
            hat = self.yh[rows, :]
            grad = out_grad(i) + norm_pull(e, self.gain(2), hat, self.yr[rows, :])
            self.gy[rows, :] = grad
            self.gyb[rows, :] = grad.astype(BF)
            return carry + fold(e * hat)

        total = blocks(t, body, fold(em * hat))
        self.small[2:3, :] = jnp.sum(total, axis=0, keepdims=True)

    def feed_forward_back(self):
        chunks = self.ff // 512

        @loop(chunks)
        def _(j):
            for n in range(2):
                cols = slice(n * 256, n * 256 + 256)
                got = dot_nt(self.gyb[...], self.w.down_rows(2 * j + n, 2 * chunks))
                self.gpre[j, :, cols] = (got * self.dg[j, :, cols].astype(F32)).astype(BF)

    def feed_forward_enter(self):
        t = self.tokens
        chunks = self.ff // 512

        @loop(2)
        def _(n):
            cols = rows_at(n, self.width // 2)
            total = dot_nt(self.gpre[0], self.w.row_part(WUP, n, 2))
            for j in range(1, chunks):
                total = total + dot_nt(self.gpre[j], self.w.row_part(WUP + j, n, 2))
            self.e[0:t, cols] = total

        def body(rows, i, carry):
            e = self.e[rows, :]
            hat = self.ah[rows, :]
            grad = self.gy[rows, :] + norm_pull(e, self.gain(1), hat, self.ar[rows, :])
            self.gy[rows, :] = grad
            self.gab[rows, :] = grad.astype(BF)
            return carry + fold(e * hat)

        total = blocks(t, body, jnp.zeros((8, self.width), F32))
        self.small[1:2, :] = jnp.sum(total, axis=0, keepdims=True)

    def project_back(self):
        heads = self.pinv.shape[0]
        inv = jnp.concatenate([self.pinv[h] for h in range(heads)], axis=0).T
        for n in range(2):
            cols = slice(n * 256, n * 256 + 256)
            block = lane_block(256, HEAD)
            scale = inv[:, 4 * n : 4 * n + 1]
            for h in range(1, 4):
                scale = jnp.where(block >= h, inv[:, 4 * n + h : 4 * n + h + 1], scale)
            self.gmx[:, cols] = (dot_nt(self.gab[...], self.w.row_part(WO, n, 2)) * scale).astype(BF)

    def attend_back(self, first, count):
        t, r = self.tokens, self.r
        span = 256

        @loop(count)
        def _(i):
            p = i + first
            cols = rows_at(p, 128)
            half = lane_block(128, HEAD)
            steps = [(hh, n) for hh in range(2) for n in range(t // span)]

            def score(j):
                hh, n = steps[j]
                qc = slice(n * span, n * span + span)
                g = self.gmx[qc, cols]
                dp = dot_nt(self.v[:, cols], jnp.where(half == hh, g, jnp.zeros_like(g)))
                self.held(j)[...] = dp
                total = jnp.sum(self.pt[2 * p + hh, :, qc].astype(F32) * dp, axis=0, keepdims=True)
                self.top[j % 2] = total * self.pinv[2 * p + hh, :, qc]

            def soften(j):
                hh, n = steps[j]
                qc = slice(n * span, n * span + span)
                e = self.pt[2 * p + hh, :, qc].astype(F32)
                self.dst[hh, :, qc] = (e * (self.held(j)[...] - self.top[j % 2])).astype(BF)

            def queries(j):
                hh, n = steps[j]
                qc = slice(n * span, n * span + span)
                feats = pl.ds(pl.multiple_of(p * 128 + hh * HEAD, HEAD), HEAD)
                got = dot(self.kt[feats, :], self.dst[hh, :, qc])
                self.dqt[feats, qc] = (got * HEAD**-0.5).astype(BF)

            def keys(hh):
                dv = dot(self.pt[2 * p + hh], self.gmx[:, cols]).astype(BF)
                dk = dot(self.dst[hh], self.q[:, cols]).astype(BF)
                if hh == 1:
                    dv = jnp.where(half == 0, self.dv[:, cols], dv)
                    dk = jnp.where(half == 0, self.dk[:, cols], dk)
                self.dv[:, cols] = dv
                self.dk[:, cols] = dk

            score(0)
            for j in range(len(steps)):
                if j + 1 < len(steps):
                    score(j + 1)
                soften(j)
                queries(j)
                if steps[j][1] == t // span - 1:
                    keys(steps[j][0])

    def queries_back(self):
        self.dq[...] = self.dqt[...].T

    def enter_back(self):
        t = self.tokens

        @loop(2)
        def _(n):
            cols = rows_at(n, self.width // 2)
            self.e[:, cols] = dot_nt(self.dk[...], self.w.row_part(WK, n, 2)) + dot_nt(
                self.dv[...], self.w.row_part(WV, n, 2)
            )
            self.e[0:t, cols] += dot_nt(self.dq[...], self.w.row_part(WQ, n, 2))

    def norm_enter(self, input_grad):
        t, r = self.tokens, self.r
        e = self.e[t:r, :]
        hat = self.xh[t:r, :]
        first = fold(e * hat)
        mem_grad = self.gm[...] * self.gate[...] + self.bwm[...]
        mem_grad = mem_grad + norm_pull(e, self.gain(0), hat, self.xr[t:r, :])

        def body(rows, i, carry):
            e = self.e[rows, :]
            hat = self.xh[rows, :]
            grad = self.gy[rows, :] + norm_pull(e, self.gain(0), hat, self.xr[rows, :])
            input_grad[rows, :] = grad.astype(BF)
            return carry + fold(e * hat)

        total = blocks(t, body, first)
        self.small[0:1, :] = jnp.sum(total, axis=0, keepdims=True)

        return mem_grad


class Packing:
    def __init__(self, shards, ctxs, width, ff):
        self.shards, self.ctxs, self.width, self.ff = shards, ctxs, width, ff
        self.head_rows = h = width // (shards * ctxs)
        self.row_rows = width // (shards * ctxs * 4)
        self.down_rows = ff // (shards * ctxs * 4)
        at = 0
        self.heads = {}
        bounds = [at]
        for name in ("uq", "uk", "uv", "uo", "ugate"):
            self.heads[name] = at
            at += h
        bounds.append(at)
        self.at_down = at
        at += self.down_rows * (width // 128)
        bounds.append(at)
        self.at_up = at
        at += self.row_rows * (ff // 128)
        bounds.append(at)
        self.at_wo = at
        at += self.row_rows * (width // 128)
        for name in ("wq", "wk", "wv"):
            self.heads[name] = at
            at += h
        self.rows = at
        bounds.append(at)
        chunks = []
        for lo, hi in zip(bounds[:-1], bounds[1:]):
            middle = lo + (hi - lo) // 2 // 16 * 16
            chunks += [(lo, middle), (middle, hi)]
        self.chunks = tuple(chunks)

    @property
    def shape(self):
        return (self.shards, self.ctxs, 2, 2, self.rows, 128)


def weight_grads(u, g, pk, names):
    width = u.width
    tile = 256

    def store_head(at, m, got):
        h = pk.head_rows
        per = tile // h
        for i in range(per):
            s = m * (per // pk.ctxs) + i // pk.ctxs
            for t in range(4):
                g[s, i % pk.ctxs, t // 2, t % 2, at : at + h, :] = got[
                    i * h : i * h + h, t * 128 : t * 128 + 128
                ]

    def store_rows(at, h, m, got, chunk0):
        per = tile // h
        for i in range(per):
            if per % (pk.ctxs * 4) == 0:
                s, c = m * (per // (pk.ctxs * 4)) + i // (pk.ctxs * 4), (i // 4) % pk.ctxs
            else:
                owner = m * (per // 4) + i // 4
                s, c = lax.div(owner, pk.ctxs), lax.rem(owner, pk.ctxs)
            for j in range(got.shape[1] // 128):
                lo = at + (chunk0 + j) * h
                g[s, c, (i // 2) % 2, i % 2, lo : lo + h, :] = got[
                    i * h : i * h + h, j * 128 : j * 128 + 128
                ]

    def heads(left, items):
        @loop(width // tile)
        def _(m):
            lt = left[:, rows_at(m, tile)].T
            for name, lo, hi, right in items:
                store_head(pk.heads[name], m, dot(lt[:, lo:hi], right[...]).astype(BF))

    t, r = u.tokens, u.r
    if "down" in names:
        for j in range(u.ff // 512):

            @loop(512 // tile)
            def _(m, j=j):
                lt = u.act[j, :, rows_at(m, tile)].T
                got = dot(lt, u.gyb[...]).astype(BF)
                store_rows(pk.at_down, pk.down_rows, m + j * (512 // tile), got, 0)

    if "up" in names:

        @loop(width // tile)
        def _(m):
            lt = u.fin[:, rows_at(m, tile)].T
            for j in range(u.ff // 512):
                store_rows(pk.at_up, pk.row_rows, m, dot(lt, u.gpre[j]).astype(BF), 4 * j)

    if "wo" in names:

        @loop(width // tile)
        def _(m):
            got = dot(u.mixt[rows_at(m, tile), :], u.gab[...]).astype(BF)
            store_rows(pk.at_wo, pk.row_rows, m, got, 0)

    if "write" in names:
        heads(u.wri, (("uq", t, r, u.dsq), ("uk", 0, r, u.dsk), ("uv", 0, r, u.dsv)))
        heads(u.gup, (("uo", 0, r - t, u.wrt),))
        heads(u.ggl, (("ugate", 0, r - t, u.wri.at[t:r]),))
    if "enter" in names:
        heads(u.enc, (("wq", 0, t, u.dq), ("wk", 0, r, u.dk), ("wv", 0, r, u.dv)))


GROUPS = ((0, 3), (3, 8), (8, 12), (12, 17))


def greet(peers):
    barrier = pltpu.get_barrier_semaphore()
    count = 0
    for cond, device in peers:

        @pl.when(cond)
        def _(device=device):
            pl.semaphore_signal(barrier, inc=1, device_id=device, device_id_type=MESH)

        count = count + jnp.where(cond, 1, 0)
    pl.semaphore_wait(barrier, count)


class Gather:
    UP, DOWN, ACROSS, BESIDE, FAR, PAIR, PAIR_ACROSS, PAIR_BESIDE, PAIR_FAR = range(9)
    LINKS = {ACROSS: 0, BESIDE: 1, FAR: 2, PAIR: 3, PAIR_ACROSS: 3, PAIR_BESIDE: 3, PAIR_FAR: 3}

    def __init__(self, shards, halved, w, send, line_send, recv, pair_recv):
        self.n, self.halved, self.w = shards, halved, w
        self.send, self.line_send, self.recv, self.pair_recv = send, line_send, recv, pair_recv
        self.s, self.c, self.t = (lax.axis_index(a) for a in ("shard", "ctx", "tp"))
        odd = lax.rem(self.t, 2)
        self.pair_tp = self.t + 1 - 2 * odd
        self.across_tp = lax.rem(self.t + 2, 4)
        self.pair = {"tp": self.pair_tp}
        self.across = {"tp": self.across_tp}
        self.beside = {"ctx": self.c + 1 - 2 * lax.rem(self.c, 2)}

    def copy(self, kind, source, tp, g, device, half=None):
        lo, hi = GROUPS[g]
        block = self.w.at[source * 4 + tp, lo:hi]
        if half is not None:
            size = self.w.shape[2] // 2
            block = self.w.at[source * 4 + tp, lo:hi, pl.ds(pl.multiple_of(half * size, size), size)]
        return self.between(block, kind, source, g, device)

    def between(self, block, kind, source, g, device):
        if kind in (self.UP, self.DOWN):
            send = self.line_send.at[kind, source]
        else:
            send = self.send.at[self.LINKS[kind]]
        to_pair = kind in (self.PAIR, self.PAIR_ACROSS, self.PAIR_BESIDE, self.PAIR_FAR)
        recv = self.pair_recv.at[g] if to_pair else self.recv.at[kind, source, g]
        return pltpu.make_async_remote_copy(
            src_ref=block, dst_ref=block, send_sem=send, recv_sem=recv, device_id=device, device_id_type=MESH,
        )

    @property
    def mine(self):
        return self.c if self.halved else None

    @property
    def others(self):
        return 1 - self.c

    def up(self, source, g, far):
        return self.copy(self.UP, source, self.t, g, {"shard": self.s + 1}, self.mine if far else None)

    def down(self, source, g, far):
        return self.copy(self.DOWN, source, self.t, g, {"shard": self.s - 1}, self.mine if far else None)

    def to_across(self, source, g, tp=None):
        return self.copy(self.ACROSS, source, self.t if tp is None else tp, g, self.across, self.mine)

    def to_pair(self, source, g, far, tp=None):
        return self.copy(self.PAIR, source, self.t if tp is None else tp, g, self.pair, self.mine if far else None)

    def far(self, d):
        return self.halved and d == self.n - 1

    def start_own(self, g):
        s, n = self.s, self.n
        if n > 1:

            @pl.when(s < n - 1)
            def _():
                self.up(s, g, self.far(1)).start()

            @pl.when(s > 0)
            def _():
                self.down(s, g, self.far(1)).start()

        self.to_across(s, g).start()
        self.to_pair(s, g, False).start()

    def came(self, source, g, d):
        self.to_across(source, g).start()
        self.to_pair(source, g, self.far(d)).start()
        if self.far(d):
            self.copy(self.FAR, source, self.t, g, self.beside, self.c).start()

    def line_step(self, d, g):
        s, n = self.s, self.n

        @pl.when(s - d >= 0)
        def _():
            self.up(s - d, g, self.far(d)).wait_recv()

            @pl.when(s < n - 1)
            def _():
                self.up(s - d, g, self.far(d + 1)).start()

            self.came(s - d, g, d)

        @pl.when(s + d <= n - 1)
        def _():
            self.down(s + d, g, self.far(d)).wait_recv()

            @pl.when(s > 0)
            def _():
                self.down(s + d, g, self.far(d + 1)).start()

            self.came(s + d, g, d)

    def sources(self, d):
        s, n = self.s, self.n
        both = ((s - d, s - d >= 0), (s + d, s + d <= n - 1))
        return both[:1] if d == 0 else both

    def across_step(self, d, g):
        for source, cond in self.sources(d):

            @pl.when(cond)
            def _(source=source):
                tp = self.across_tp
                self.to_across(source, g, tp).wait_recv()
                self.copy(self.PAIR_ACROSS, source, tp, g, self.pair, self.mine).start()
                if self.halved:
                    self.copy(self.BESIDE, source, tp, g, self.beside, self.c).start()

    def beside_step(self, d, g):
        if not self.halved:
            return
        for source, cond in self.sources(d):

            @pl.when(cond)
            def _(source=source):
                tp = self.across_tp
                self.copy(self.BESIDE, source, tp, g, self.beside, self.others).wait_recv()
                self.copy(self.PAIR_BESIDE, source, tp, g, self.pair, self.others).start()

    def far_step(self, g):
        if not self.halved:
            return
        for source, cond in self.sources(self.n - 1):

            @pl.when(cond)
            def _(source=source):
                self.copy(self.FAR, source, self.t, g, self.beside, self.others).wait_recv()
                self.copy(self.PAIR_FAR, source, self.t, g, self.pair, self.others).start()

    def finish(self, g):
        lo, hi = GROUPS[g]
        self.between(self.w.at[0 : 2 * self.n, lo:hi], self.PAIR, 0, g, self.pair).wait_recv()

    def drain(self):
        s, n = self.s, self.n
        parts = n // 2 if self.halved else n
        half = self.w.at[0, :, 0 : self.w.shape[2] // 2]
        self.between(self.w.at[0 : 2 * n], self.PAIR, 0, 0, self.pair).wait_send()
        self.between(self.w.at[0:parts], self.ACROSS, 0, 0, self.across).wait_send()
        if self.halved:
            self.between(self.w.at[0:parts], self.BESIDE, 0, 0, self.beside).wait_send()

            @pl.when(jnp.logical_or(s == 0, s == n - 1))
            def _():
                self.between(half, self.FAR, 0, 0, self.beside).wait_send()

        for d in range(n - 1):
            block = half if self.far(d + 1) else self.w.at[0]

            @pl.when(jnp.logical_and(s - d >= 0, s < n - 1))
            def _(d=d, block=block):
                self.between(block, self.UP, s - d, 0, {"shard": s + 1}).wait_send()

            @pl.when(jnp.logical_and(s + d <= n - 1, s > 0))
            def _(d=d, block=block):
                self.between(block, self.DOWN, s + d, 0, {"shard": s - 1}).wait_send()

    def events(self, time, ready, between):
        n = self.n
        groups = range(len(GROUPS))
        for g in groups:
            if time == max(g - 1, 0):
                ready(g)
                self.start_own(g)
        for g in groups:
            d = time - g
            if not 1 <= d <= n + 1:
                continue
            if d <= n - 1:
                self.line_step(d, g)
            if d <= n:
                self.across_step(d - 1, g)
            if d >= 2:
                self.beside_step(d - 2, g)
            if d == n + 1:
                self.far_step(g)
                self.finish(g)
            between(time - n - 1 if g >= time - n - 1 else -1)

    @property
    def last(self):
        return (len(GROUPS) - 1) + self.n + 1


def line_peers(n):
    s = lax.axis_index("shard")
    return [(s >= 0, {"shard": lax.rem(s + d, n)}) for d in range(1, n)]


def tp_peers():
    t = lax.axis_index("tp")
    return [(t >= 0, {"tp": lax.rem(t + d, 4)}) for d in (1, 2, 3)]


def own_tiles(weights, w, own, sems):
    names = [WQ, WK, WV, WO, WUP, WDOWN, UQ, UK, UV, UO, UGATE]
    rows = w.shape[2]
    out = []
    for name, ref in zip(names, weights):
        parts = {WUP: 4, WDOWN: 4}.get(name, 1)
        for j in range(parts):
            src = ref
            if name == WUP:
                src = ref.at[:, j * 512 : j * 512 + 512]
            if name == WDOWN:
                src = ref.at[j * rows : j * rows + rows]
            out.append(pltpu.make_async_copy(src, w.at[own, name + j], sems.at[name + j]))
    return out


class Reduce:
    ORDER = (0, 2, 0, 1, 0, 1, 0, 1)

    def __init__(self, shards, chunks, g, r1, r2, r3, z, zfirst, send, recv):
        self.n = shards
        self.sizes = [hi - lo for lo, hi in chunks]
        self.rows = [pl.ds(lo, hi - lo) for lo, hi in chunks]
        self.g, self.r1, self.r2, self.r3, self.z = g, r1, r2, r3, z
        self.zz, self.zx, self.zy, self.zsend, self.zrecv = zfirst
        self.send, self.recv = send, recv
        self.s, self.c, self.t = (lax.axis_index(a) for a in ("shard", "ctx", "tp"))
        self.core = lax.rem(self.t, 2)
        self.x = lax.div(self.t, 2)
        self.pair = {"tp": self.t + 1 - 2 * self.core}
        self.across = {"tp": lax.rem(self.t + 2, 4)}
        self.beside = {"ctx": 1 - self.c}

    def early(self, k, step):
        rows = self.rows[k]
        if step < self.n - 1:
            to = lax.rem(self.s + step + 1, self.n)
            src, dst, device = self.r1.at[to, :, :, rows], self.zz.at[step], {"shard": to}
        elif step == self.n - 1:
            src, dst, device = self.r1.at[self.s, :, 1 - self.x, rows], self.zx, self.across
        else:
            src, dst, device = self.zx.at[1 - self.c], self.zy, self.beside
        return pltpu.make_async_remote_copy(
            src_ref=src, dst_ref=dst, send_sem=self.zsend.at[step], recv_sem=self.zrecv.at[step],
            device_id=device, device_id_type=MESH,
        )

    def copy(self, src, dst, k, kind, device):
        return pltpu.make_async_remote_copy(
            src_ref=src, dst_ref=dst, send_sem=self.send.at[kind], recv_sem=self.recv.at[k, kind],
            device_id=device, device_id_type=MESH,
        )

    def one(self, k):
        rows = self.rows[k]
        return self.copy(self.g.at[:, :, :, 1 - self.core, rows], self.r1.at[:, :, :, rows], k, 0, self.pair)

    def two(self, k):
        rows = self.rows[k]
        if self.ORDER[k] == 0:
            src, device = self.r1.at[:, :, 1 - self.x, rows], self.across
        else:
            src, device = self.r1.at[:, 1 - self.c, :, rows], self.beside
        return self.copy(src, self.r2.at[:, :, rows], k, 1, device)

    def three(self, k):
        rows = self.rows[k]
        if self.ORDER[k] == 0:
            src, device = self.r2.at[:, 1 - self.c, rows], self.beside
        else:
            src, device = self.r2.at[:, 1 - self.x, rows], self.across
        return self.copy(src, self.r3.at[:, rows], k, 2, device)

    def along(self, k, d):
        to = lax.rem(self.s + d, self.n)
        rows = self.rows[k]
        return self.copy(self.r3.at[to, rows], self.z.at[d - 1, rows], k, 2 + d, {"shard": to})

    def start(self, k):
        self.one(k).start()

    def to_second(self, k):
        self.one(k).wait_recv()
        rows = self.rows[k]
        for j in range(2):
            for x in range(2):
                self.r1[:, j, x, rows] += self.g[:, j, x, self.core, rows]
        if self.ORDER[k] == 2:
            for step in range(self.n - 1):
                self.early(k, step).start()
            return
        self.two(k).start()

    def to_third(self, k):
        rows = self.rows[k]
        if self.ORDER[k] == 2:
            for step in range(self.n - 1):
                self.early(k, step).wait_recv()
            for j in range(2):
                for x in range(2):
                    total = self.r1[self.s, j, x, rows].astype(F32)
                    for step in range(self.n - 1):
                        total = total + self.zz[step, j, x].astype(F32)
                    self.r1[self.s, j, x, rows] = total.astype(BF)
            self.early(k, self.n - 1).start()
            return
        self.two(k).wait_recv()
        for j in range(2):
            own = self.r1[:, j, self.x, rows] if self.ORDER[k] == 0 else self.r1[:, self.c, j, rows]
            self.r2[:, j, rows] += own
        self.three(k).start()

    def to_last(self, k):
        rows = self.rows[k]
        if self.ORDER[k] == 2:
            self.early(k, self.n - 1).wait_recv()
            for j in range(2):
                self.zx[j] += self.r1[self.s, j, self.x, rows]
            self.early(k, self.n).start()
            return
        self.three(k).wait_recv()
        own = self.c if self.ORDER[k] == 0 else self.x
        self.r3[:, rows] += self.r2[:, own, rows]
        for d in range(1, self.n):
            self.along(k, d).start()

    def arrive(self, k, out):
        rows = self.rows[k]
        if self.ORDER[k] == 2:
            self.early(k, self.n).wait_recv()
            out[rows, :] = (self.zx[self.c].astype(F32) + self.zy[...].astype(F32)).astype(out.dtype)
            return
        for d in range(1, self.n):
            self.along(k, d).wait_recv()
        total = self.r3[self.s, rows].astype(F32)
        for d in range(1, self.n):
            total = total + self.z[d - 1, rows].astype(F32)
        out[rows, :] = total.astype(out.dtype)

    def drain(self):
        first = self.ORDER.index(2)
        rest = sum(self.sizes) - self.sizes[first]
        whole = [(self.r1, 0), (self.r1.at[:, :, 0, 0:rest], 1), (self.r1.at[:, 0, 0, 0:rest], 2)]
        whole += [(self.r3.at[0, 0:rest], 2 + d) for d in range(1, self.n)]
        for ref, kind in whole:
            self.copy(ref, ref, 0, kind, self.pair).wait_send()
        for step in range(self.n + 1):
            self.early(first, step).wait_send()


class SmallSum:
    def __init__(self, shards, own, got, send, recv):
        self.n, self.own, self.got, self.send, self.recv = shards, own, got, send, recv
        self.s, self.c, self.t = (lax.axis_index(a) for a in ("shard", "ctx", "tp"))

    def copy(self, i):
        near = [{"tp": self.t + 1 - 2 * lax.rem(self.t, 2)}, {"tp": lax.rem(self.t + 2, 4)}, {"ctx": 1 - self.c}]
        device = near[i] if i < 3 else {"shard": lax.rem(self.s + i - 2, self.n)}
        return pltpu.make_async_remote_copy(
            src_ref=self.own.at[min(i, 3)], dst_ref=self.got.at[i], send_sem=self.send.at[i],
            recv_sem=self.recv.at[i], device_id=device, device_id_type=MESH,
        )

    def start(self, value):
        self.own[0] = value
        self.copy(0).start()

    def step(self, i):
        self.copy(i).wait_recv()
        self.own[i + 1] = self.own[i] + self.got[i]
        if i < 2:
            self.copy(i + 1).start()
        else:
            for d in range(1, self.n):
                self.copy(2 + d).start()

    def arrive(self, out):
        total = self.own[3]
        for d in range(1, self.n):
            self.copy(2 + d).wait_recv()
            total = total + self.got[2 + d]
        out[...] = total

    def drain(self):
        for i in range(2 + self.n):
            self.copy(i).wait_send()


class Spread:
    def __init__(self, src, dst, send, recv):
        self.src, self.dst, self.send, self.recv = src, dst, send, recv
        self.t = lax.axis_index("tp")

    def copy(self, d):
        to = lax.rem(self.t + d, 4)
        share = self.dst.shape[1]
        src = self.src.at[pl.ds(pl.multiple_of(to * share, share), share)]
        dst = self.dst.at[self.t]
        if d == 0:
            return pltpu.make_async_copy(src, dst, self.send.at[d])
        return pltpu.make_async_remote_copy(
            src_ref=src, dst_ref=dst, send_sem=self.send.at[d], recv_sem=self.recv.at[d],
            device_id={"tp": to}, device_id_type=MESH,
        )

    def start(self):
        for d in (2, 3, 1, 0):
            self.copy(d).start()

    def finish(self):
        for d in (1, 2, 3):
            self.copy(d).wait_recv()
            self.copy(d).wait_send()
        self.copy(0).wait()


class Share:
    def __init__(self, held, send, recv):
        self.held, self.send, self.recv = held, send, recv
        self.t = lax.axis_index("tp")
        self.pair_tp = self.t + 1 - 2 * lax.rem(self.t, 2)
        self.across_tp = lax.rem(self.t + 2, 4)

    def copy(self, i, tp, to):
        return pltpu.make_async_remote_copy(
            src_ref=self.held.at[tp], dst_ref=self.held.at[tp], send_sem=self.send.at[i],
            recv_sem=self.recv.at[i], device_id={"tp": to}, device_id_type=MESH,
        )

    def start(self):
        self.copy(0, self.t, self.across_tp).start()
        self.copy(1, self.t, self.pair_tp).start()

    def relay(self):
        self.copy(0, self.across_tp, self.across_tp).wait_recv()
        self.copy(2, self.across_tp, self.pair_tp).start()

    def finish(self):
        self.copy(1, self.pair_tp, self.pair_tp).wait_recv()
        self.copy(2, lax.rem(self.pair_tp + 2, 4), self.pair_tp).wait_recv()
        self.copy(0, self.t, self.across_tp).wait_send()
        self.copy(1, self.t, self.pair_tp).wait_send()
        self.copy(2, self.across_tp, self.pair_tp).wait_send()


class Comm:
    pass


def step_scratch(shards, pk, direct, tokens, slots, width):
    v, dma = pltpu.VMEM, pltpu.SemaphoreType.DMA
    n = shards
    out = dict(
        w=v((n * 4, TILES, width // (n * 4), width), BF),
        x=v((tokens, width), BF),
        m0=v((slots, width), F32),
        og=v((4, tokens // 4, width), BF),
        y=v((tokens, width), BF),
        xg=v((tokens, width), BF),
        mems=v((4, slots, width), BF),
        migs=v((4, slots, width), BF),
        small=v((8, width), F32),
        m_send=v((slots, width), BF),
        m_recv=v((slots, width), BF),
        g_send=v((slots, width), BF),
        g_recv=v((slots, width), BF),
        chain=dma((4,)),
        loads=dma((3,)),
        local=dma((TILES,)),
        w_send=dma((4,)),
        w_line_send=dma((2, n)),
        w_recv=dma((5, n, len(GROUPS))),
        w_pair_recv=dma((len(GROUPS),)),
        og_send=dma((4,)),
        og_recv=dma((4,)),
        y_send=dma((4,)),
        y_recv=dma((4,)),
        xg_send=dma((4,)),
        xg_recv=dma((4,)),
        mem_send=dma((3,)),
        mem_recv=dma((3,)),
        mig_send=dma((3,)),
        mig_recv=dma((3,)),
    )
    if direct:
        c = len(pk.chunks)
        lo, hi = pk.chunks[Reduce.ORDER.index(2)]
        early = hi - lo
        out.update(
            g=v(pk.shape, BF),
            r1=v((n, 2, 2, pk.rows, 128), BF),
            r2=v((n, 2, pk.rows, 128), BF),
            r3=v((n, pk.rows, 128), BF),
            z=v((n - 1, pk.rows, 128), BF),
            zz=v((n - 1, 2, 2, early, 128), BF),
            zx=v((2, early, 128), BF),
            zy=v((early, 128), BF),
            zsend=dma((n + 1,)),
            zrecv=dma((n + 1,)),
            own=v((4, 8, width), F32),
            got=v((2 + n, 8, width), F32),
            r_send=dma((2 + n,)),
            r_recv=dma((c, 2 + n)),
            s_send=dma((2 + n,)),
            s_recv=dma((2 + n,)),
        )
    return out


def step_kernel(dims, pk, direct, names, unit_names, *refs):
    shards, ctxs, halved = dims
    first, length, inputs, first_memory, memory_grad, out_grad = refs[:6]
    weights, gains, outs = refs[6:17], refs[17:21], refs[21:27]
    scratch = refs[27:]
    b = Comm()
    b.__dict__.update(zip(names, scratch))
    unit_refs = dict(zip(unit_names, scratch[len(names) :]))
    if not direct:
        b.g = outs[4]
    s, c, t = (lax.axis_index(a) for a in ("shard", "ctx", "tp"))
    u = Unit(unit_refs, Weights(b.w), b.x, gains, b.small)

    loads = [
        pltpu.make_async_copy(inputs.at[t], b.x, b.loads.at[0]),
        pltpu.make_async_copy(first_memory.at[t], b.m0, b.loads.at[1]),
        pltpu.make_async_copy(memory_grad.at[t], u.gm, b.loads.at[2]),
    ]
    copies = own_tiles(weights, b.w, s * 4 + t, b.local)
    for copy in copies + loads:
        copy.start()
    mine = pltpu.make_async_copy(out_grad.at[t], b.og.at[t], b.og_send.at[0])
    mine.start()
    peers = line_peers(shards) + tp_peers()
    if ctxs > 1:
        peers += [(c > 0, {"ctx": c - 1}), (c < ctxs - 1, {"ctx": c + 1})]
    greet(peers)
    gather = Gather(shards, halved, b.w, b.w_send, b.w_line_send, b.w_recv, b.w_pair_recv)

    def ready(g):
        for copy in copies[GROUPS[g][0] : GROUPS[g][1]]:
            copy.wait()

    lead, follow = pl.when(c == 0), pl.when(c > 0)
    pairs = u.width // 128
    chunks = u.ff // 512

    def on_lead(*calls):
        def run():
            @lead
            def _():
                for call in calls:
                    call()

        return run

    def take_memory():
        u.mem[...] = b.m0[...]
        u.memory_in()
        u.attend_memory()

    def project_and_attend():
        u.project_tokens()
        u.attend(0, 1)

    work = [(0, project_and_attend)]
    work += [(0, partial(u.attend, p, 1)) for p in range(1, pairs)]
    work += [
        (0, on_lead(take_memory)),
        (1, on_lead(u.after_attention)),
        (1, on_lead(partial(u.feed_forward_up, 0, chunks // 2))),
        (1, on_lead(partial(u.feed_forward_up, chunks // 2, chunks - chunks // 2))),
        (2, on_lead(u.feed_forward_down)),
    ]

    def between(complete):
        if work and work[0][0] <= complete:
            work.pop(0)[1]()

    def chain_copy(i, to):
        src, dst = ((b.m_send, b.m_recv), (b.g_send, b.g_recv))[i]
        return pltpu.make_async_remote_copy(
            src_ref=src, dst_ref=dst, send_sem=b.chain.at[2 * i], recv_sem=b.chain.at[2 * i + 1],
            device_id={"ctx": to}, device_id_type=MESH,
        )

    def og_copy(d):
        to = lax.rem(t + d, 4)
        return pltpu.make_async_remote_copy(
            src_ref=out_grad.at[to], dst_ref=b.og.at[t], send_sem=b.og_send.at[d],
            recv_sem=b.og_recv.at[d], device_id={"tp": to}, device_id_type=MESH,
        )

    spread_y = Spread(b.y, outs[0], b.y_send, b.y_recv)
    spread_xg = Spread(b.xg, outs[2], b.xg_send, b.xg_recv)
    share_mem = Share(b.mems, b.mem_send, b.mem_recv)
    share_mig = Share(b.migs, b.mig_send, b.mig_recv)
    gather.events(0, ready, between)
    for copy in loads:
        copy.wait()
    u.make_bias(first[0, t], length[0, t])
    gather.events(1, ready, between)
    u.tokens_in()
    for time in range(2, gather.last + 1):
        gather.events(time, ready, between)
    while work:
        work.pop(0)[1]()
    for d in (1, 2, 3):
        og_copy(d).start()

    if ctxs > 1:

        @follow
        def _():
            gather.drain()
            chain_copy(0, c - 1).wait_recv()
            u.mem[...] = b.m_recv[...].astype(F32)
            u.memory_in()
            u.attend_memory()
            u.after_attention()
            u.feed_forward_up(0, chunks)
            u.feed_forward_down()

    after = u.write_memory()
    b.m_send[...] = after.astype(BF)
    if ctxs > 1:

        @pl.when(c < ctxs - 1)
        def _():
            chain_copy(0, c + 1).start()

    b.mems[t] = after.astype(BF)
    b.y[...] = u.af[0 : u.tokens, :].astype(BF)
    share_mem.start()
    spread_y.start()
    u.backward_early()
    mine.wait()
    for d in (1, 2, 3):
        og_copy(d).wait_recv()
    share_mem.relay()

    @lead
    def _():
        gather.drain()

    if ctxs > 1:

        @pl.when(c < ctxs - 1)
        def _():
            chain_copy(1, c + 1).wait_recv()
            u.gm[...] += b.g_recv[...].astype(F32)

    def out_grad_rows(i):
        per = b.og.shape[1] // BLOCK
        return b.og[lax.div(i, per), pl.ds(lax.rem(i, per) * BLOCK, BLOCK), :].astype(F32)

    def grads(*which):
        weight_grads(u, b.g, pk, which)

    red = None
    if direct:
        early = (b.zz, b.zx, b.zy, b.zsend, b.zrecv)
        red = Reduce(shards, pk.chunks, b.g, b.r1, b.r2, b.r3, b.z, early, b.r_send, b.r_recv)
    sums = SmallSum(shards, b.own, b.got, b.s_send, b.s_recv) if direct else None
    WRITE, DOWN, UP, ENTER = (0, 1), (2, 3), (4, 5), (6, 7)

    def reduce(*todo):
        for what, chunks in todo if direct else ():
            for k in chunks:
                getattr(red, what)(k, *((outs[4],) if what == "arrive" else ()))

    u.write_back()

    @lead
    def _():
        grads("write")
        reduce(("start", WRITE))

    u.write_enter(out_grad_rows)

    @lead
    def _():
        grads("down")
        reduce(("start", DOWN), ("to_second", WRITE))

    u.feed_forward_back()

    @lead
    def _():
        grads("up")
        reduce(("start", UP), ("to_second", DOWN))

    u.feed_forward_enter()

    @lead
    def _():
        grads("wo")
        reduce(("to_second", UP))

    u.project_back()
    u.attend_back(0, pairs // 2)

    @lead
    def _():
        reduce(("to_third", WRITE))

    u.attend_back(pairs // 2, pairs - pairs // 2)
    u.queries_back()

    @lead
    def _():
        grads("enter")
        reduce(("start", ENTER), ("to_third", DOWN))

    u.enter_back()

    @lead
    def _():
        reduce(("to_second", ENTER), ("to_third", UP), ("to_last", WRITE))

    back = u.norm_enter(b.xg)
    b.migs[t] = back.astype(BF)

    if ctxs > 1:

        @follow
        def _():
            b.g_send[...] = back.astype(BF)
            chain_copy(1, c - 1).start()
            grads("write")
            reduce(("start", WRITE))
            grads("down")
            reduce(("start", DOWN))
            grads("up")
            reduce(("start", UP), ("to_second", WRITE))
            grads("wo", "enter")
            reduce(("start", ENTER), ("to_second", DOWN), ("to_second", UP), ("to_second", ENTER))

    share_mig.start()
    if direct:
        sums.start(b.small[...])

    def sum_step(i):
        if direct:
            sums.step(i)

    @lead
    def _():
        sum_step(0)
        reduce(("to_third", ENTER))
        spread_xg.start()
        reduce(("to_last", DOWN), ("to_last", UP))
        sum_step(1)

    if ctxs > 1:

        @follow
        def _():
            sum_step(0)
            spread_xg.start()
            reduce(("to_third", (0, 2, 4, 6)), ("to_third", (1, 3, 5)))
            sum_step(1)
            reduce(("to_last", WRITE), ("to_last", DOWN), ("to_third", (7,)), ("to_last", UP))

    share_mig.relay()
    reduce(("to_last", ENTER))
    sum_step(2)

    for spread in (spread_y, share_mem):
        spread.finish()
    reduce(*(("arrive", pair) for pair in (WRITE, DOWN, UP)))
    for spread in (share_mig, spread_xg):
        spread.finish()
    kept = [
        pltpu.make_async_copy(b.mems, outs[1], b.loads.at[0]),
        pltpu.make_async_copy(b.migs, outs[3], b.loads.at[1]),
    ]
    for copy in kept:
        copy.start()
    for d in (1, 2, 3):
        og_copy(d).wait_send()
    if ctxs > 1:

        @pl.when(c < ctxs - 1)
        def _():
            chain_copy(0, c + 1).wait_send()

        @pl.when(c > 0)
        def _():
            chain_copy(1, c - 1).wait_send()

    if direct:
        sums.arrive(outs[5])
        reduce(("arrive", ENTER))
        sums.drain()
        red.drain()
    else:
        outs[5][...] = b.small[...]
    for copy in kept:
        copy.wait()


def run_step(dims, pk, direct, first, length, inputs, first_memory, memory_grad, out_grad, weights, gains):
    _, tokens, width = inputs.shape
    slots = first_memory.shape[1]
    vm = pl.BlockSpec(memory_space=pltpu.VMEM)
    sm = pl.BlockSpec(memory_space=pltpu.SMEM)
    hbm = pl.BlockSpec(memory_space=pl.ANY)
    scratch = step_scratch(dims[0], pk, direct, tokens, slots, width)
    unit = unit_scratch(tokens, slots, width, pk.ff)
    shape = jax.ShapeDtypeStruct
    return pl.pallas_call(
        partial(step_kernel, dims, pk, direct, tuple(scratch), tuple(unit)),
        out_shape=(
            shape((4, tokens // 4, width), BF), shape((4, slots, width), BF),
            shape((4, tokens // 4, width), BF), shape((4, slots, width), BF),
            shape((pk.rows, 128) if direct else pk.shape, BF), shape((8, width), F32),
        ),
        in_specs=[sm, sm] + [hbm] * 15 + [vm] * 4,
        out_specs=(hbm, hbm, hbm, hbm, vm, vm),
        scratch_shapes=list(scratch.values()) + list(unit.values()),
        compiler_params=pltpu.CompilerParams(
            vmem_limit_bytes=VMEM_LIMIT, collective_id=1, has_side_effects=True
        ),
        name="step",
    )(first, length, inputs, first_memory, memory_grad, out_grad, *weights, *gains)


def store_kernel(pk, owners, *refs):
    rows_in, total, small = refs[:4], refs[4], refs[5]
    rows_out, (wq, wk, wv, wo, up, down, uq, uk, uv, uo, ugate), vectors = refs[6:10], refs[10:21], refs[21:]
    for src, dst in zip(rows_in, rows_out):
        dst[...] = src[...].astype(dst.dtype)

    def part(at, size):
        return total[at : at + size, :].astype(F32)

    h = pk.head_rows
    for name, ref in dict(wq=wq, wk=wk, wv=wv, uq=uq, uk=uk, uv=uv).items():
        ref[...] = part(pk.heads[name], h)
    for name, ref in dict(uo=uo, ugate=ugate).items():
        ref[...] = part(pk.heads[name], h)
    for at, r, ref in ((pk.at_wo, pk.row_rows, wo), (pk.at_up, pk.row_rows, up), (pk.at_down, pk.down_rows, down)):
        for j in range(ref.shape[1] // 128):
            ref[:, j * 128 : j * 128 + 128] = part(at + j * r, r)
    share = small.shape[1] // owners
    owner = lax.axis_index("shard")
    for axis in ("ctx", "tp"):
        owner = owner * lax.axis_size(axis) + lax.axis_index(axis)
    turned = pltpu.roll(small[...], small.shape[1] - owner * share, 1)
    for i, ref in enumerate(vectors):
        ref[...] = turned[i : i + 1, 0:share]


def run_store(pk, owners, rows, total, small):
    vm = pl.BlockSpec(memory_space=pltpu.VMEM)
    shape = jax.ShapeDtypeStruct
    width = small.shape[1]
    h = pk.head_rows
    head = shape((h, 128), F32)
    outs = tuple(shape(r.shape, d) for r, d in zip(rows, (BF, F32, BF, F32))) + (
        head, head, head, shape((pk.row_rows, width), F32), shape((pk.row_rows, pk.ff), F32),
        shape((pk.down_rows, width), F32), head, head, head, head, head,
    ) + (shape((1, width // owners), F32),) * 4
    return pl.pallas_call(
        partial(store_kernel, pk, owners),
        out_shape=outs,
        in_specs=[vm] * 6,
        out_specs=(vm,) * len(outs),
        compiler_params=pltpu.CompilerParams(vmem_limit_bytes=VMEM_LIMIT),
        name="store",
    )(*rows, total, small)


def full_gradients(pk, grads):
    groups, owners = pk.shards * pk.ctxs, pk.shards * pk.ctxs * 4
    by_head = grads.reshape(groups, 4, pk.rows, 128)
    by_owner = grads.reshape(owners, pk.rows, 128)

    def head(name):
        at = pk.heads[name]
        got = by_head[:, :, at : at + pk.head_rows]
        return got.transpose(0, 2, 1, 3).reshape(pk.width, pk.width).astype(F32)

    def rows(at, h, n):
        got = by_owner[:, at : at + h * n].reshape(owners, n, h, 128)
        return got.transpose(0, 2, 1, 3).reshape(owners * h, n * 128).astype(F32)

    return (
        head("wq"), head("wk"), head("wv"),
        rows(pk.at_wo, pk.row_rows, pk.width // 128),
        rows(pk.at_up, pk.row_rows, pk.ff // 128),
        rows(pk.at_down, pk.down_rows, pk.width // 128),
        head("uq"), head("uk"), head("uv"), head("uo").T, head("ugate").T,
    )


def local(
    inputs, first_memory, piece_start, piece_len,
    w_query, w_key, w_value, w_out, w_up, w_down, u_query, u_key, u_value, u_out, u_gate,
    gain_attn, gain_ffn, gain_write, gate_bias, out_grad, memory_grad,
):
    shards, ctxs, tps = (lax.axis_size(a) for a in ("shard", "ctx", "tp"))
    seqs, tokens, width = inputs.shape
    ff = w_up.shape[1]
    assert seqs == tps == 4 and tokens == width == 512 and ff == 2048
    weights = (w_query, w_key, w_value, w_out, w_up, w_down, u_query, u_key, u_value, u_out, u_gate)
    gains = [v.reshape(1, -1) for v in (gain_attn, gain_ffn, gain_write, gate_bias)]
    owners = shards * ctxs * tps
    direct = ctxs == 2 and width % (owners * 16) == 0
    halved = ctxs == 2 and w_query.shape[0] % 32 == 0
    pk = Packing(shards if direct else 4, 2, width, ff)
    got = run_step(
        (shards, ctxs, halved), pk, direct, piece_start.T, piece_len.T, inputs, first_memory, memory_grad,
        out_grad, weights, gains,
    )
    if direct:
        out = run_store(pk, owners, got[:4], got[4], got[5])
        return out[:13] + (out[13].T, out[14].T) + tuple(v.reshape(-1) for v in out[15:])
    every = ("shard", "ctx", "tp")
    out = [got[0], got[1].astype(F32), got[2], got[3].astype(F32)]
    for i, g in enumerate(full_gradients(pk, got[4])):
        if i in (3, 4, 5):
            out.append(lax.psum_scatter(g, every, scatter_dimension=0, tiled=True))
            continue
        sum_dim = 1 if i >= 9 else 0
        cut = lax.psum_scatter(g, "tp", scatter_dimension=1 - sum_dim, tiled=True)
        out.append(lax.psum_scatter(cut, ("shard", "ctx"), scatter_dimension=sum_dim, tiled=True))
    for i in range(4):
        out.append(lax.psum_scatter(got[5][i], every, scatter_dimension=0, tiled=True))
    return tuple(out)


def solution(mesh):
    cut = P(("shard", "tp"), None)
    head, rows, turned = P(("shard", "ctx"), "tp"), P(("shard", "ctx", "tp"), None), P("tp", ("shard", "ctx"))
    vector = P(("shard", "ctx", "tp"))
    over_rows, over_ctx = P("shard", ("ctx", "tp"), None), P("shard", "ctx", None)
    return jax.shard_map(
        local,
        mesh=mesh,
        in_specs=(over_ctx, P("shard", None, None), P("shard", "ctx"), P("shard", "ctx"))
        + (cut,) * 11 + (P(),) * 4 + (over_rows, over_ctx),
        out_specs=(over_rows, over_ctx, over_rows, over_ctx)
        + (head,) * 3 + (rows,) * 3 + (head,) * 3 + (turned,) * 2 + (vector,) * 4,
        check_vma=False,
    )
```

profile of v0, /device:TPU:0, one launch (start us, length us, event | category | flops | bytes accessed | tf_op | source)
XLA Modules:
  0.0 160.0 jit_solution(8661768849583793708)
XLA Ops:
  0.7 156.1 %step.1 = (bf16[4,128,512]{2,1,0:T(8,128)(2,1)}, bf16[4,64,512]{2,1,0:T(8,128)(2,1)}, bf16[4,128,512]{2,1,0:T(8,128)(2,1)}, bf16[4,64,512]{2,1,0:T(8,128)(2,1)},...) custom-call(s32[1,4]{1,0:T(1,128)} %bitcast.16, s32[1,4]{1,0:T(1,128)} %bitcast.17, bf16[4,512,512]{2,1,0:T(8,128)(2,1)} %refs_2_.1, ...), custom_call_target="tpu_custom_call" | custom-call | tf_op jit(solution)/shard_map/step/pallas_call | solution.py:1534
  156.8 3.0 %store.1 = (bf16[4,128,512]{2,1,0:T(8,128)(2,1)}, f32[4,64,512]{2,1,0:T(8,128)}, bf16[4,128,512]{2,1,0:T(8,128)(2,1)}, f32[4,64,512]{2,1,0:T(8,128)}, f32[64,128...) custom-call(bf16[4,128,512]{2,1,0:T(8,128)(2,1)} %get-tuple-element., ...), custom_call_target="tpu_custom_call" | custom-call | tf_op jit(solution)/shard_map/store/pallas_call | solution.py:1587
where the time goes:
time: 160 us
  Pallas kernels  159 us (99%)
    pallas_call x1, Pallas kernels, run_step(): pl.pallas_call(partial(step_kernel, dims, pk, direct, tuple(scratch), tup...  156 us

commit v1 on v0

--- a/solution.py
+++ b/solution.py
@@ -155,6 +155,7 @@
         gy=v((tokens, width), F32),
         gyb=v((tokens, width), BF),
         bwm=v((slots, width), F32),
+        folded=v((8, width), F32),
         gpre=v((ff // 512, tokens, 512), BF),
         gab=v((tokens, width), BF),
         gmx=v((tokens, width), BF),
@@ -558,12 +559,23 @@
                 if j + 1 < len(steps):
                     score(j + 1)
                 soften(j)
+                if j == len(steps) - 2:
+                    keys(0)
                 queries(j)
-                if steps[j][1] == t // span - 1:
-                    keys(steps[j][0])
+            keys(1)
 
     def queries_back(self):
         self.dq[...] = self.dqt[...].T
+
+    def enter_memory(self):
+        t, r = self.tokens, self.r
+        e = dot_nt(self.dk[t:r, :], self.w.row_part(WK, 0, 1)) + dot_nt(
+            self.dv[t:r, :], self.w.row_part(WV, 0, 1)
+        )
+        hat = self.xh[t:r, :]
+        self.folded[...] = fold(e * hat)
+        back = self.gm[...] * self.gate[...] + self.bwm[...]
+        return back + norm_pull(e, self.gain(0), hat, self.xr[t:r, :])
 
     def enter_back(self):
         t = self.tokens
@@ -571,18 +583,14 @@
         @loop(2)
         def _(n):
             cols = rows_at(n, self.width // 2)
-            self.e[:, cols] = dot_nt(self.dk[...], self.w.row_part(WK, n, 2)) + dot_nt(
-                self.dv[...], self.w.row_part(WV, n, 2)
+            self.e[0:t, cols] = (
+                dot_nt(self.dk[0:t, :], self.w.row_part(WK, n, 2))
+                + dot_nt(self.dv[0:t, :], self.w.row_part(WV, n, 2))
+                + dot_nt(self.dq[...], self.w.row_part(WQ, n, 2))
             )
-            self.e[0:t, cols] += dot_nt(self.dq[...], self.w.row_part(WQ, n, 2))
 
     def norm_enter(self, input_grad):
-        t, r = self.tokens, self.r
-        e = self.e[t:r, :]
-        hat = self.xh[t:r, :]
-        first = fold(e * hat)
-        mem_grad = self.gm[...] * self.gate[...] + self.bwm[...]
-        mem_grad = mem_grad + norm_pull(e, self.gain(0), hat, self.xr[t:r, :])
+        t = self.tokens
 
         def body(rows, i, carry):
             e = self.e[rows, :]
@@ -591,10 +599,8 @@
             input_grad[rows, :] = grad.astype(BF)
             return carry + fold(e * hat)
 
-        total = blocks(t, body, first)
+        total = blocks(t, body, self.folded[...])
         self.small[0:1, :] = jnp.sum(total, axis=0, keepdims=True)
-
-        return mem_grad
 
 
 class Packing:
@@ -1427,6 +1433,15 @@
         reduce(("to_third", WRITE))
 
     u.attend_back(pairs // 2, pairs - pairs // 2)
+    back = u.enter_memory()
+    b.migs[t] = back.astype(BF)
+    if ctxs > 1:
+
+        @follow
+        def _():
+            b.g_send[...] = back.astype(BF)
+            chain_copy(1, c - 1).start()
+
     u.queries_back()
 
     @lead
@@ -1440,15 +1455,12 @@
     def _():
         reduce(("to_second", ENTER), ("to_third", UP), ("to_last", WRITE))
 
-    back = u.norm_enter(b.xg)
-    b.migs[t] = back.astype(BF)
+    u.norm_enter(b.xg)
 
     if ctxs > 1:
 
         @follow
         def _():
-            b.g_send[...] = back.astype(BF)
-            chain_copy(1, c - 1).start()
             grads("write")
             reduce(("start", WRITE))
             grads("down")

time: 160 us -> 158 us (0.988)
  Pallas kernels: 159 us -> 157 us
    pallas_call x1, Pallas kernels: 156 us -> 154 us  [run_step(): pl.pallas_call(partial(step_kernel, dims, pk, direct, tuple(scratch), tup...]
where the time goes in v1:
time: 158 us
  Pallas kernels  157 us (99%)
    pallas_call x1, Pallas kernels, run_step(): pl.pallas_call(partial(step_kernel, dims, pk, direct, tuple(scratch), tup...  154 us

profile of v1, /device:TPU:0, one launch (start us, length us, event | category | flops | bytes accessed | tf_op | source)
XLA Modules:
  0.0 157.8 jit_solution(2475226514445031836)
XLA Ops:
  0.7 153.9 %step.1 = (bf16[4,128,512]{2,1,0:T(8,128)(2,1)}, bf16[4,64,512]{2,1,0:T(8,128)(2,1)}, bf16[4,128,512]{2,1,0:T(8,128)(2,1)}, bf16[4,64,512]{2,1,0:T(8,128)(2,1)},...) custom-call(s32[1,4]{1,0:T(1,128)} %bitcast.16, s32[1,4]{1,0:T(1,128)} %bitcast.17, bf16[4,512,512]{2,1,0:T(8,128)(2,1)} %refs_2_.1, ...), custom_call_target="tpu_custom_call" | custom-call | tf_op jit(solution)/shard_map/step/pallas_call | solution.py:1546
  154.6 3.0 %store.1 = (bf16[4,128,512]{2,1,0:T(8,128)(2,1)}, f32[4,64,512]{2,1,0:T(8,128)}, bf16[4,128,512]{2,1,0:T(8,128)(2,1)}, f32[4,64,512]{2,1,0:T(8,128)}, f32[64,128...) custom-call(bf16[4,128,512]{2,1,0:T(8,128)(2,1)} %get-tuple-element., ...), custom_call_target="tpu_custom_call" | custom-call | tf_op jit(solution)/shard_map/store/pallas_call | solution.py:1599
